TPU v7x, 32 devices: a whole 2x2x4 slice. The times are simulated.
32 devices in a mesh: groups: 2 (over y), seq: 4 (over z), head: 2 (over x), sub: 2 (over core).
Axes of the slice: x: 2, y: 2, z: 4, core: 2. Of those that a mesh axis runs over, the one named last changes fastest.
Arguments:
- inputs: bfloat16 [16384, 1536], P(('groups', 'seq'), ('head', 'sub')), parts along dimension 0, may hold values from -6 to 6
- b_proj: bfloat16 [16384, 128], P(('groups', 'seq')), parts along dimension 0, may hold values from -0.109375 to 0.109375
- c_proj: bfloat16 [16384, 128], P(('groups', 'seq')), parts along dimension 0, may hold values from -6 to 6
- step_codes: int32 [24, 16384], P(('head', 'sub'), ('groups', 'seq')), parts along dimension 1, may hold values from 0 to 3
- gate_codes: int32 [16384], P(('groups', 'seq')), parts along dimension 0, may hold values from 0 to 2
- decay_rates: float32 [24], P(('head', 'sub')), may hold values from 1.8310547e-05 to 0.12
- skip_gain: float32 [24], P(('head', 'sub')), may hold values from 0.5 to 1.5
- conv_weight: float32 [4, 1536], P(None, ('head', 'sub')), may hold values from -3 to 3
- out_cotangent: bfloat16 [16384, 1536], P(('groups', 'seq'), ('head', 'sub')), parts along dimension 0, may hold values from -6 to 6
Outputs:
- layer_out: bfloat16 [16384, 1536], P(('groups', 'seq'), ('head', 'sub')), parts along dimension 0
- input_grad: bfloat16 [16384, 1536], P(('groups', 'seq'), ('head', 'sub')), parts along dimension 0
- conv_grad: float32 [8, 1536], P('groups', ('head', 'sub')), parts along dimension 0
There are 2 independent parts, one for each index of `groups`. A program takes and returns all parts, laid end to end along the dimension named above; an argument that names none is the same for every part. Nothing has to cross between parts.
All inputs are finite; a program needn't handle non-finite values.
Results may differ from a plain program's by a relative error of at most 0.0062.
Values may be sent and summed in bfloat16 or wider, within the bound.
No kernel may reach another device: no remote copies, remote signals or barrier semaphores. Data moves between devices by JAX's collectives and lax.ppermute only.
A program may use at most 64 MiB of HBM per device.

v0:
```python
import jax
import jax.numpy as jnp
from jax import lax
from jax.sharding import PartitionSpec as P

BLOCK = 512


def shifted(block, axis, distance):
    devices = range(lax.axis_size(axis))
    route = [(i - distance, i) for i in devices if i - distance in devices]
    return lax.ppermute(block, axis, route)


def shards(
    inputs,
    b_proj,
    c_proj,
    step_codes,
    gate_codes,
    decay_rates,
    skip_gain,
    conv_weight,
    out_cotangent,
):
    row_count, channels = inputs.shape
    conv_taps = conv_weight.shape[0]
    head_count = decay_rates.shape[0]
    head_width = channels // head_count
    state_width = b_proj.shape[1]
    block_count = row_count // BLOCK
    highest = lax.Precision.HIGHEST
    before_rows = shifted(inputs[row_count - (conv_taps - 1) :], "seq", 1)
    padded = jnp.concatenate([before_rows, inputs], axis=0)
    preact = jnp.zeros((row_count, channels), jnp.float32)
    for offset in range(conv_taps):
        preact = preact + conv_weight[offset] * padded[offset : offset + row_count].astype(
            jnp.float32
        )
    mixed_in = jax.nn.silu(preact).astype(jnp.bfloat16)
    step_size = jnp.exp2(-step_codes.astype(jnp.float32))
    log_decay = (
        -decay_rates[:, None] * step_size
        + jnp.log(1.0 - gate_codes.astype(jnp.float32) / 4.0)[None, :]
    )
    cum_decay = jnp.cumsum(log_decay.reshape(head_count, block_count, BLOCK), axis=-1).transpose(
        1, 0, 2
    )
    step_blocks = step_size.reshape(head_count, block_count, BLOCK).transpose(1, 0, 2)
    mixed_blocks = mixed_in.reshape(block_count, BLOCK, head_count, head_width)
    grad_blocks = out_cotangent.reshape(block_count, BLOCK, head_count, head_width)
    b_blocks = b_proj.reshape(block_count, BLOCK, state_width)
    c_blocks = c_proj.reshape(block_count, BLOCK, state_width)
    causal = jnp.arange(BLOCK)[:, None] >= jnp.arange(BLOCK)[None, :]

    def local_block(unused, block_data):
        mixed_b, grad_b, b_block, c_block, cum_block, step_block = block_data
        scores = jnp.dot(c_block, b_block.T, preferred_element_type=jnp.float32)
        spread = cum_block[:, :, None] - cum_block[:, None, :]
        decays = jnp.exp(jnp.where(causal[None], spread, -jnp.inf))
        weights = (scores[None] * decays * step_block[:, None, :]).astype(jnp.bfloat16)
        ahead_part = jnp.einsum(
            "hts,shp->thp", weights, mixed_b, preferred_element_type=jnp.float32
        )
        behind_part = jnp.einsum(
            "hst,shp->thp", weights, grad_b, preferred_element_type=jnp.float32
        )
        block_total = cum_block[:, -1]
        in_factor = (jnp.exp(block_total[:, None] - cum_block) * step_block).T
        scaled_in = (mixed_b.astype(jnp.float32) * in_factor[:, :, None]).astype(jnp.bfloat16)
        fresh_state = jnp.einsum(
            "thp,tn->hpn", scaled_in, b_block, preferred_element_type=jnp.float32
        )
        scaled_out = (grad_b.astype(jnp.float32) * jnp.exp(cum_block).T[:, :, None]).astype(
            jnp.bfloat16
        )
        fresh_adjoint = jnp.einsum(
            "thp,tn->hpn", scaled_out, c_block, preferred_element_type=jnp.float32
        )
        return (unused, (ahead_part, behind_part, fresh_state, fresh_adjoint))

    unused_carry, block_results = lax.scan(
        local_block,
        jnp.zeros((), jnp.float32),
        (mixed_blocks, grad_blocks, b_blocks, c_blocks, cum_decay, step_blocks),
    )
    ahead_parts, behind_parts, fresh_states, fresh_adjoints = block_results
    block_totals = cum_decay[:, :, -1]
    zero_state = jnp.zeros((head_count, head_width, state_width), jnp.float32)
    running = zero_state
    start_list = []
    for block_index in range(block_count):
        start_list.append(running)
        running = (
            jnp.exp(block_totals[block_index])[:, None, None] * running + fresh_states[block_index]
        )
    local_end = running
    running = zero_state
    later_list = []
    for block_index in range(block_count - 1, -1, -1):
        later_list.append(running)
        running = (
            jnp.exp(block_totals[block_index])[:, None, None] * running
            + fresh_adjoints[block_index]
        )
    end_list = later_list[::-1]
    device_total = jnp.sum(block_totals, axis=0)
    totals_all = lax.all_gather(device_total[None], "seq", axis=0, tiled=True)
    position = lax.axis_index("seq")
    prefix = jnp.cumsum(totals_all, axis=0) - totals_all
    own_prefix = lax.dynamic_slice_in_dim(prefix, position, 1, 0)[0]
    end_pieces = lax.all_gather(local_end[None], "seq", axis=0, tiled=True)
    start_pieces = lax.all_gather(running[None], "seq", axis=0, tiled=True)
    piece_count = end_pieces.shape[0]
    sources = jnp.arange(piece_count, dtype=jnp.int32)
    from_below = (sources < position)[:, None]
    from_above = (sources > position)[:, None]
    forward_weight = jnp.exp(
        jnp.where(from_below, own_prefix[None] - prefix - totals_all, -jnp.inf)
    )
    backward_weight = jnp.exp(
        jnp.where(from_above, prefix - own_prefix[None] - device_total[None], -jnp.inf)
    )
    forward_sum = jnp.einsum("jh,jhpn->hpn", forward_weight, end_pieces, precision=highest)
    backward_sum = jnp.einsum("jh,jhpn->hpn", backward_weight, start_pieces, precision=highest)
    before_blocks = jnp.cumsum(block_totals, axis=0) - block_totals
    after_blocks = device_total[None] - jnp.cumsum(block_totals, axis=0)
    start_states = jnp.exp(before_blocks)[:, :, None, None] * forward_sum[None] + jnp.stack(
        start_list
    )
    end_adjoints = jnp.exp(after_blocks)[:, :, None, None] * backward_sum[None] + jnp.stack(
        end_list
    )
    carried_out = jnp.einsum(
        "btn,bhpn->bthp",
        c_blocks,
        start_states.astype(jnp.bfloat16),
        preferred_element_type=jnp.float32,
    )
    carried_out = carried_out * jnp.exp(cum_decay).transpose(0, 2, 1)[..., None]
    skip_wide = skip_gain[None, None, :, None]
    layer_out = (skip_wide * mixed_blocks.astype(jnp.float32) + ahead_parts + carried_out).astype(
        jnp.bfloat16
    )
    layer_out = layer_out.reshape(row_count, channels)
    back_factor = (step_blocks * jnp.exp(block_totals[:, :, None] - cum_decay)).transpose(0, 2, 1)
    carried_back = jnp.einsum(
        "btn,bhpn->bthp",
        b_blocks,
        end_adjoints.astype(jnp.bfloat16),
        preferred_element_type=jnp.float32,
    )
    carried_back = carried_back * back_factor[..., None]
    grad_in = (skip_wide * grad_blocks.astype(jnp.float32) + behind_parts + carried_back).reshape(
        row_count, channels
    )
    gate_value = jax.nn.sigmoid(preact)
    grad_pre = grad_in * gate_value * (1.0 + preact * (1.0 - gate_value))
    after_rows = shifted(grad_pre[: conv_taps - 1], "seq", -1)
    extended = jnp.concatenate([grad_pre, after_rows], axis=0)
    input_grad = jnp.zeros((row_count, channels), jnp.float32)
    for offset in range(conv_taps):
        shift_from = conv_taps - 1 - offset
        input_grad = (
            input_grad + conv_weight[offset] * extended[shift_from : shift_from + row_count]
        )
    tap_sums = [
        jnp.sum(grad_pre * padded[offset : offset + row_count].astype(jnp.float32), axis=0)
        for offset in range(conv_taps)
    ]
    local_grad = jnp.stack(tap_sums)
    conv_grad = lax.psum(local_grad, "seq") * (row_count * lax.axis_size("seq")) ** (-0.5)
    return (layer_out, input_grad.astype(jnp.bfloat16), conv_grad)


def solution(mesh):
    in_specs = (
        P(("groups", "seq"), ("head", "sub")),
        P(("groups", "seq"), None),
        P(("groups", "seq"), None),
        P(("head", "sub"), ("groups", "seq")),
        P(("groups", "seq")),
        P(("head", "sub")),
        P(("head", "sub")),
        P(None, ("head", "sub")),
        P(("groups", "seq"), ("head", "sub")),
    )
    out_specs = (
        P(("groups", "seq"), ("head", "sub")),
        P(("groups", "seq"), ("head", "sub")),
        P("groups", ("head", "sub")),
    )
    return jax.shard_map(shards, mesh=mesh, in_specs=in_specs, out_specs=out_specs, check_vma=False)
```

profile of v0, /device:TPU:0, one launch (start us, length us, event | category | flops | bytes accessed | tf_op | source)
XLA Modules:
  0.0 186.4 jit_solution(6552634328493133739)
XLA Ops:
  0.6 0.8 slice.104
  1.5 0.8 copy.102
  2.2 4.9 %collective-permute-start = (bf16[3,384]{0,1:T(8,128)(2,1)}, bf16[3,384]{0,1:T(8,128)(2,1)S(1)}, u32[]{:S(2)}, u32[]{:S(2)}) collective-permute-start(bf16[3,384]{0,1:T(8,128)(2,1)} %copy.102), channel_id=1, source_target_pairs={{0,4},{4,8},{8,12},{1,5},{5,9},{9,13},{2,6},{6,10},{10,14},{3,7},{... | collective-permute-start | bytes 6920 | tf_op jit(solution)/shard_map/ppermute | solution.py:12
  7.2 0.7 subtract_log_fusion
  7.9 0.7 neg.13
  8.5 0.9 multiply_exponential_fusion
  9.5 7.2 %reduce-window.6 = f32[6,4,4,128]{3,2,1,0:T(4,128)S(1)} reduce-window(f32[6,4,4,128]{3,2,1,0:T(4,128)S(1)} %reshape.125, f32[]{:T(128)} %constant.51.clone.1), window={size=1x1x1x128 pad=0_0x0_0x0_0x127_0}, to_apply=%region_0.1 | reduce-window | flops 1560576 | bytes 98308 | tf_op jit(solution)/shard_map/reduce-window
  16.8 0.2 copy.106
  17.3 0.8 fusion.73
  18.1 0.2 fusion.80
  18.6 1.2 dynamic-slice
  20.5 0.2 dynamic-update-slice
  20.7 9.9 %all-reduce = f32[24]{0:T(128)S(1)} all-reduce(f32[24]{0:T(128)S(1)} %dynamic-update-slice), channel_id=2, replica_groups=mesh['groups'=2,'seq'=4,'head'=2,'sub'=2] {'seq'}, use_global_device_ids=true, to_apply=%add | all-reduce | flops 24 | bytes 192
  30.8 0.6 broadcast_multiply_fusion.1
  31.6 0.9 slice_reduce_fusion.3
  32.4 1.7 copy.103
  34.2 1.7 copy.108
  35.9 2.9 %reshape.128 = bf16[4,512,6,64]{1,0,3,2:T(4,128)(2,1)S(1)} reshape(bf16[2048,384]{0,1:T(8,128)(2,1)} %copy.108) | data formatting | bytes 3145728 | tf_op jit(solution)/shard_map/reshape | solution.py:51
  38.8 1.7 copy.112
  40.7 4.2 %multiply_convert_fusion.13 = (bf16[2048,384]{0,1:T(8,128)(2,1)}, f32[2048,384]{0,1:T(8,128)}) fusion(bf16[2048,384]{0,1:T(8,128)(2,1)S(1)} %copy.103, f32[384]{0:T(512)S(1)} %get-tuple-element.162, bf16[3,384]{0,1:T(8,128)(2,1)S(1)} %collective-permute-done, f32[384]{0:T(512)S(1)} %get-tuple-element.163, f32[384]{0:T(512)S(1)} %get-tuple-element.161, ...), kind=kLoop, calls=%fused_computation.84 | loop fusion | flops 19660800 | bytes 6299904 | tf_op jit(solution)/shard_map/convert_element_type | solution.py:40
  44.9 2.9 %reshape.122 = bf16[4,512,6,64]{1,0,3,2:T(4,128)(2,1)S(1)} reshape(bf16[2048,384]{0,1:T(8,128)(2,1)} %get-tuple-element.195) | data formatting | bytes 3145728 | tf_op jit(solution)/shard_map/reshape | solution.py:50
  47.9 1.5 copy.105
  49.4 55.1 %while.17 = (s32[]{:T(128)}, f32[4,512,6,64]{1,3,2,0:T(8,128)}, f32[4,512,6,64]{1,3,2,0:T(8,128)}, f32[4,6,64,128]{3,2,1,0:T(8,128)}, f32[4,6,64,128]{3,2,1,0:T(...) while((s32[]{:T(128)}, f32[4,512,6,64]{1,3,2,0:T(8,128)}, ...), condition=%wide.region_3.4_spmd.clone, body=%wide.region_2.3_spmd.clone.sunk | while | flops 587601920 | bytes 8374465 | solution.py:82
  49.4 1.2 fusion.106
  50.8 3.9 %fusion.108 = f32[4,512,6,64]{1,3,2,0:T(8,128)} fusion(f32[4,512,6,64]{1,3,2,0:T(8,128)} %get-tuple-element.310, s32[]{:T(128)} %get-tuple-element.308, f32[6,512]{1,0:T(8,128)S(1)} %bitcast.175, f32[6,512]{1,0:T(8,128)S(1)} %bitcast.177, f32[512,512]{1,0:T(8,128)S(1)} %fusion.106, pred[512,512]{1,0:T(8,128)(4,1)S(1)} %iota_compare_fusion.4, ...), kind=kOutput, calls=%fused_computation.7.clone.1 | convolution fusion | flops 209190912 | bytes 2540544 | tf_op jit(solution)/shard_map/while/body/eval_jaxpr/hst,shp->thp/dot_general | solution.py:65
  54.7 3.9 %fusion.107 = f32[4,512,6,64]{1,3,2,0:T(8,128)} fusion(f32[4,512,6,64]{1,3,2,0:T(8,128)} %get-tuple-element.309, s32[]{:T(128)} %get-tuple-element.308, f32[6,512]{1,0:T(8,128)S(1)} %bitcast.176, f32[6,512]{1,0:T(8,128)S(1)} %bitcast.178, f32[512,512]{1,0:T(8,128)S(1)} %fusion.106, pred[512,512]{1,0:T(8,128)(4,1)S(1)} %iota_compare_fusion.4, ...), kind=kOutput, calls=%fused_computation.5.clone.1 | convolution fusion | flops 209190912 | bytes 2540544 | tf_op jit(solution)/shard_map/while/body/eval_jaxpr/hts,shp->thp/dot_general | solution.py:62
  58.7 0.1 copy.155
  59.1 2.0 %fusion.109 = f32[4,6,64,128]{3,2,1,0:T(8,128)} fusion(f32[4,6,64,128]{3,2,1,0:T(8,128)} %get-tuple-element.311, s32[]{:T(128)} %get-tuple-element.308, f32[512,6]{0,1:T(8,128)S(1)} %copy.156, bf16[4,512,6,64]{1,3,2,0:T(8,128)(2,1)} %get-tuple-element.325, bf16[4,512,128]{2,1,0:T(8,128)(2,1)} %get-tuple-element.327), kind=kOutput, calls=%fused_computation.11.clone.1 | convolution fusion | flops 50921472 | bytes 734720 | tf_op jit(solution)/shard_map/while/body/eval_jaxpr/thp,tn->hpn/dot_general | solution.py:71
  61.2 2.0 %fusion.110 = f32[4,6,64,128]{3,2,1,0:T(8,128)} fusion(f32[4,6,64,128]{3,2,1,0:T(8,128)} %get-tuple-element.312, s32[]{:T(128)} %get-tuple-element.308, f32[512,6]{0,1:T(8,128)S(1)} %copy.157, bf16[4,512,6,64]{1,3,2,0:T(8,128)(2,1)} %get-tuple-element.330, bf16[4,512,128]{2,1,0:T(8,128)(2,1)S(1)} %get-tuple-element.326), kind=kOutput, calls=%fused_computation.9.clone.1 | convolution fusion | flops 50921472 | bytes 738816 | tf_op jit(solution)/shard_map/while/body/eval_jaxpr/thp,tn->hpn/dot_general | solution.py:77
  63.1 1.2 fusion.106
  64.5 3.9 %fusion.108 = f32[4,512,6,64]{1,3,2,0:T(8,128)} fusion(f32[4,512,6,64]{1,3,2,0:T(8,128)} %get-tuple-element.310, s32[]{:T(128)} %get-tuple-element.308, f32[6,512]{1,0:T(8,128)S(1)} %bitcast.175, f32[6,512]{1,0:T(8,128)S(1)} %bitcast.177, f32[512,512]{1,0:T(8,128)S(1)} %fusion.106, pred[512,512]{1,0:T(8,128)(4,1)S(1)} %iota_compare_fusion.4, ...), kind=kOutput, calls=%fused_computation.7.clone.1 | convolution fusion | flops 209190912 | bytes 2540544 | tf_op jit(solution)/shard_map/while/body/eval_jaxpr/hst,shp->thp/dot_general | solution.py:65
  68.4 3.9 %fusion.107 = f32[4,512,6,64]{1,3,2,0:T(8,128)} fusion(f32[4,512,6,64]{1,3,2,0:T(8,128)} %get-tuple-element.309, s32[]{:T(128)} %get-tuple-element.308, f32[6,512]{1,0:T(8,128)S(1)} %bitcast.176, f32[6,512]{1,0:T(8,128)S(1)} %bitcast.178, f32[512,512]{1,0:T(8,128)S(1)} %fusion.106, pred[512,512]{1,0:T(8,128)(4,1)S(1)} %iota_compare_fusion.4, ...), kind=kOutput, calls=%fused_computation.5.clone.1 | convolution fusion | flops 209190912 | bytes 2540544 | tf_op jit(solution)/shard_map/while/body/eval_jaxpr/hts,shp->thp/dot_general | solution.py:62
  72.8 2.0 %fusion.109 = f32[4,6,64,128]{3,2,1,0:T(8,128)} fusion(f32[4,6,64,128]{3,2,1,0:T(8,128)} %get-tuple-element.311, s32[]{:T(128)} %get-tuple-element.308, f32[512,6]{0,1:T(8,128)S(1)} %copy.156, bf16[4,512,6,64]{1,3,2,0:T(8,128)(2,1)} %get-tuple-element.325, bf16[4,512,128]{2,1,0:T(8,128)(2,1)} %get-tuple-element.327), kind=kOutput, calls=%fused_computation.11.clone.1 | convolution fusion | flops 50921472 | bytes 734720 | tf_op jit(solution)/shard_map/while/body/eval_jaxpr/thp,tn->hpn/dot_general | solution.py:71
  74.9 2.0 %fusion.110 = f32[4,6,64,128]{3,2,1,0:T(8,128)} fusion(f32[4,6,64,128]{3,2,1,0:T(8,128)} %get-tuple-element.312, s32[]{:T(128)} %get-tuple-element.308, f32[512,6]{0,1:T(8,128)S(1)} %copy.157, bf16[4,512,6,64]{1,3,2,0:T(8,128)(2,1)} %get-tuple-element.330, bf16[4,512,128]{2,1,0:T(8,128)(2,1)S(1)} %get-tuple-element.326), kind=kOutput, calls=%fused_computation.9.clone.1 | convolution fusion | flops 50921472 | bytes 738816 | tf_op jit(solution)/shard_map/while/body/eval_jaxpr/thp,tn->hpn/dot_general | solution.py:77
  76.8 1.2 fusion.106
  78.2 4.0 %fusion.108 = f32[4,512,6,64]{1,3,2,0:T(8,128)} fusion(f32[4,512,6,64]{1,3,2,0:T(8,128)} %get-tuple-element.310, s32[]{:T(128)} %get-tuple-element.308, f32[6,512]{1,0:T(8,128)S(1)} %bitcast.175, f32[6,512]{1,0:T(8,128)S(1)} %bitcast.177, f32[512,512]{1,0:T(8,128)S(1)} %fusion.106, pred[512,512]{1,0:T(8,128)(4,1)S(1)} %iota_compare_fusion.4, ...), kind=kOutput, calls=%fused_computation.7.clone.1 | convolution fusion | flops 209190912 | bytes 2540544 | tf_op jit(solution)/shard_map/while/body/eval_jaxpr/hst,shp->thp/dot_general | solution.py:65
  82.1 3.9 %fusion.107 = f32[4,512,6,64]{1,3,2,0:T(8,128)} fusion(f32[4,512,6,64]{1,3,2,0:T(8,128)} %get-tuple-element.309, s32[]{:T(128)} %get-tuple-element.308, f32[6,512]{1,0:T(8,128)S(1)} %bitcast.176, f32[6,512]{1,0:T(8,128)S(1)} %bitcast.178, f32[512,512]{1,0:T(8,128)S(1)} %fusion.106, pred[512,512]{1,0:T(8,128)(4,1)S(1)} %iota_compare_fusion.4, ...), kind=kOutput, calls=%fused_computation.5.clone.1 | convolution fusion | flops 209190912 | bytes 2540544 | tf_op jit(solution)/shard_map/while/body/eval_jaxpr/hts,shp->thp/dot_general | solution.py:62
  86.6 2.0 %fusion.109 = f32[4,6,64,128]{3,2,1,0:T(8,128)} fusion(f32[4,6,64,128]{3,2,1,0:T(8,128)} %get-tuple-element.311, s32[]{:T(128)} %get-tuple-element.308, f32[512,6]{0,1:T(8,128)S(1)} %copy.156, bf16[4,512,6,64]{1,3,2,0:T(8,128)(2,1)} %get-tuple-element.325, bf16[4,512,128]{2,1,0:T(8,128)(2,1)} %get-tuple-element.327), kind=kOutput, calls=%fused_computation.11.clone.1 | convolution fusion | flops 50921472 | bytes 734720 | tf_op jit(solution)/shard_map/while/body/eval_jaxpr/thp,tn->hpn/dot_general | solution.py:71
  88.7 2.0 %fusion.110 = f32[4,6,64,128]{3,2,1,0:T(8,128)} fusion(f32[4,6,64,128]{3,2,1,0:T(8,128)} %get-tuple-element.312, s32[]{:T(128)} %get-tuple-element.308, f32[512,6]{0,1:T(8,128)S(1)} %copy.157, bf16[4,512,6,64]{1,3,2,0:T(8,128)(2,1)} %get-tuple-element.330, bf16[4,512,128]{2,1,0:T(8,128)(2,1)S(1)} %get-tuple-element.326), kind=kOutput, calls=%fused_computation.9.clone.1 | convolution fusion | flops 50921472 | bytes 738816 | tf_op jit(solution)/shard_map/while/body/eval_jaxpr/thp,tn->hpn/dot_general | solution.py:77
  90.6 1.2 fusion.106
  92.0 4.0 %fusion.108 = f32[4,512,6,64]{1,3,2,0:T(8,128)} fusion(f32[4,512,6,64]{1,3,2,0:T(8,128)} %get-tuple-element.310, s32[]{:T(128)} %get-tuple-element.308, f32[6,512]{1,0:T(8,128)S(1)} %bitcast.175, f32[6,512]{1,0:T(8,128)S(1)} %bitcast.177, f32[512,512]{1,0:T(8,128)S(1)} %fusion.106, pred[512,512]{1,0:T(8,128)(4,1)S(1)} %iota_compare_fusion.4, ...), kind=kOutput, calls=%fused_computation.7.clone.1 | convolution fusion | flops 209190912 | bytes 2540544 | tf_op jit(solution)/shard_map/while/body/eval_jaxpr/hst,shp->thp/dot_general | solution.py:65
  96.0 3.9 %fusion.107 = f32[4,512,6,64]{1,3,2,0:T(8,128)} fusion(f32[4,512,6,64]{1,3,2,0:T(8,128)} %get-tuple-element.309, s32[]{:T(128)} %get-tuple-element.308, f32[6,512]{1,0:T(8,128)S(1)} %bitcast.176, f32[6,512]{1,0:T(8,128)S(1)} %bitcast.178, f32[512,512]{1,0:T(8,128)S(1)} %fusion.106, pred[512,512]{1,0:T(8,128)(4,1)S(1)} %iota_compare_fusion.4, ...), kind=kOutput, calls=%fused_computation.5.clone.1 | convolution fusion | flops 209190912 | bytes 2540544 | tf_op jit(solution)/shard_map/while/body/eval_jaxpr/hts,shp->thp/dot_general | solution.py:62
  100.4 2.0 %fusion.109 = f32[4,6,64,128]{3,2,1,0:T(8,128)} fusion(f32[4,6,64,128]{3,2,1,0:T(8,128)} %get-tuple-element.311, s32[]{:T(128)} %get-tuple-element.308, f32[512,6]{0,1:T(8,128)S(1)} %copy.156, bf16[4,512,6,64]{1,3,2,0:T(8,128)(2,1)} %get-tuple-element.325, bf16[4,512,128]{2,1,0:T(8,128)(2,1)} %get-tuple-element.327), kind=kOutput, calls=%fused_computation.11.clone.1 | convolution fusion | flops 50921472 | bytes 734720 | tf_op jit(solution)/shard_map/while/body/eval_jaxpr/thp,tn->hpn/dot_general | solution.py:71
  102.5 1.9 %fusion.110 = f32[4,6,64,128]{3,2,1,0:T(8,128)} fusion(f32[4,6,64,128]{3,2,1,0:T(8,128)} %get-tuple-element.312, s32[]{:T(128)} %get-tuple-element.308, f32[512,6]{0,1:T(8,128)S(1)} %copy.157, bf16[4,512,6,64]{1,3,2,0:T(8,128)(2,1)} %get-tuple-element.330, bf16[4,512,128]{2,1,0:T(8,128)(2,1)S(1)} %get-tuple-element.326), kind=kOutput, calls=%fused_computation.9.clone.1 | convolution fusion | flops 50921472 | bytes 738816 | tf_op jit(solution)/shard_map/while/body/eval_jaxpr/thp,tn->hpn/dot_general | solution.py:77
  104.5 1.8 slice_add_fusion
  106.3 17.3 %all_gather.11 = f32[4,6,64,128]{3,2,1,0:T(8,128)S(1)} all-gather(f32[1,6,64,128]{3,2,1,0:T(8,128)S(1)} %get-tuple-element.187), channel_id=1, replica_groups=mesh['groups'=2,'seq'=4,'head'=2,'sub'=2] {'seq'}, dimensions={0}, use_global_device_ids=true | all-gather | bytes 983040 | tf_op jit(solution)/shard_map/all_gather | solution.py:113
  123.6 1.8 fusion.62
  125.5 2.2 %fusion.55 = f32[4,512,6,64]{1,3,2,0:T(8,128)S(1)} fusion(f32[4,512,6,64]{1,3,2,0:T(8,128)S(1)} %copy-done.7, bf16[4,512,128,1]{2,1,3,0:T(8,128)(2,1)} %bitcast.19, f32[4,512,6]{1,2,0:T(8,128)S(1)} %copy.118, f32[6]{0:T(128)S(1)} %copy-done.17, f32[1,6,64,128]{3,2,1,0:T(8,128)S(1)} %broadcast.73, f32[1,6,64,128]{3,2,1,0:T(8,128)S(1)} %get-tuple-element.190, ...), kind=kOutput, calls=%fused_computation.79 | convolution fusion | flops 206438400 | bytes 9420920 | tf_op jit(solution)/shard_map/btn,bhpn->bthp/dot_general | solution.py:147
  127.7 2.0 %copy.119 = f32[4,512,6,64]{1,0,3,2:T(4,128)S(1)} copy(f32[4,512,6,64]{1,3,2,0:T(8,128)S(1)} %fusion.55) | data formatting | bytes 6291456 | tf_op jit(solution)/shard_map/add | solution.py:154
  129.7 1.5 copy.135
  131.2 0.9 copy-done.5
  132.1 4.2 %fusion.50 = (f32[384]{0:T(512)S(1)}, f32[384]{0:T(512)S(1)}, f32[384]{0:T(512)S(1)}, f32[384]{0:T(512)S(1)}, f32[2048,384]{0,1:T(8,128)}) fusion(bf16[2048,384]{0,1:T(8,128)(2,1)S(1)} %copy-done.1, bf16[3,384]{0,1:T(8,128)(2,1)S(1)} %collective-permute-done, f32[2048,384]{0,1:T(8,128)S(1)} %copy-done.5, f32[2048,384]{0,1:T(8,128)S(1)} %bitcast.164), kind=kLoop, calls=%fused_computation.72 | loop fusion | flops 22804992 | bytes 11018496 | tf_op jit(solution)/shard_map/reduce_sum | solution.py:168
  136.3 10.1 %psum.7 = f32[4,384]{1,0:T(4,128)S(1)} all-reduce(f32[4,384]{1,0:T(4,128)S(1)} %pad_maximum_fusion.2), channel_id=1, replica_groups=mesh['groups'=2,'seq'=4,'head'=2,'sub'=2] {'seq'}, use_global_device_ids=true, to_apply=%region_11.12 | all-reduce | flops 1536 | bytes 12288 | tf_op jit(solution)/shard_map/psum | solution.py:172
  146.5 1.6 slice.143
  148.1 1.3 collective-permute-start.1
  149.4 18.7 %all_gather.10 = f32[4,6,64,128]{3,2,1,0:T(8,128)S(1)} all-gather(f32[1,6,64,128]{3,2,1,0:T(8,128)S(1)} %get-tuple-element.211), channel_id=1, replica_groups=mesh['groups'=2,'seq'=4,'head'=2,'sub'=2] {'seq'}, dimensions={0}, use_global_device_ids=true | all-gather | bytes 983040 | tf_op jit(solution)/shard_map/all_gather | solution.py:112
  168.0 1.8 fusion.64
  169.9 3.0 %fusion.57 = bf16[4,512,6,64]{1,3,2,0:T(8,128)(2,1)S(1)} fusion(f32[4,512,6,64]{1,3,2,0:T(8,128)} %get-tuple-element.68, bf16[4,512,128,1]{2,1,3,0:T(8,128)(2,1)S(1)} %bitcast.166, f32[4,512,6]{1,2,0:T(8,128)S(1)} %copy.114, f32[6]{0:T(128)S(1)} %copy-done.17, f32[1,6,64,128]{3,2,1,0:T(8,128)S(1)} %get-tuple-element.212, ...), kind=kOutput, calls=%fused_computation.82 | convolution fusion | flops 207224832 | bytes 7848056 | tf_op jit(solution)/shard_map/btn,bhpn->bthp/dot_general | solution.py:134
  172.8 0.6 broadcast_multiply_fusion
  173.4 1.2 copy.115
  174.6 1.6 copy.134
  176.2 2.6 %copy.120 = bf16[2048,384]{1,0:T(8,128)(2,1)} copy(bf16[2048,384]{0,1:T(8,128)(2,1)} %bitcast.168) | data formatting | bytes 3145728
  178.8 5.0 %fusion.44 = bf16[2048,384]{0,1:T(8,128)(2,1)} fusion(f32[2048,384]{0,1:T(8,128)S(1)} %copy-done.4, f32[3,384]{0,1:T(8,128)S(1)} %collective-permute-done.1, f32[384]{0:T(512)S(1)} %get-tuple-element.162, f32[384]{0:T(512)S(1)} %get-tuple-element.163, f32[384]{0:T(512)S(1)} %get-tuple-element.161, f32[384]{0:T(512)S(1)} %get-tuple-element.160), kind=kLoop, calls=%fused_computation.66 | loop fusion | flops 8650752 | bytes 4729344 | tf_op jit(solution)/shard_map/convert_element_type | solution.py:173
  183.8 2.6 %copy.121 = bf16[2048,384]{1,0:T(8,128)(2,1)} copy(bf16[2048,384]{0,1:T(8,128)(2,1)} %fusion.44) | data formatting | bytes 3145728
  (109 shorter events, 4.0 us)
Async XLA Ops:
  0.6 33.6 %copy-start.8 = (bf16[2048,384]{1,0:T(8,128)(2,1)S(1)}, bf16[2048,384]{1,0:T(8,128)(2,1)}, u32[]{:S(2)}) copy-start(bf16[2048,384]{1,0:T(8,128)(2,1)} %param.19) | copy-start | bytes 4718596
  2.2 38.4 %collective-permute-start = (bf16[3,384]{0,1:T(8,128)(2,1)}, bf16[3,384]{0,1:T(8,128)(2,1)S(1)}, u32[]{:S(2)}, u32[]{:S(2)}) collective-permute-start(bf16[3,384]{0,1:T(8,128)(2,1)} %copy.102), channel_id=1, source_target_pairs={{0,4},{4,8},{8,12},{1,5},{5,9},{9,13},{2,6},{6,10},{10,14},{3,7},{... | collective-permute-start | bytes 6920 | tf_op jit(solution)/shard_map/ppermute | solution.py:12
  18.1 13.4 %copy-start.9 = (f32[6]{0:T(128)}, f32[6]{0:T(128)S(1)}, u32[]{:S(2)}) copy-start(f32[6]{0:T(128)S(1)} %get-tuple-element.156) | copy-start | bytes 76
  18.1 13.4 %copy-start.11 = (f32[6]{0:T(128)}, f32[6]{0:T(128)S(1)}, u32[]{:S(2)}) copy-start(f32[6]{0:T(128)S(1)} %get-tuple-element.157) | copy-start | bytes 76
  34.2 6.5 %copy-start = (bf16[2048,384]{0,1:T(8,128)(2,1)}, bf16[2048,384]{0,1:T(8,128)(2,1)S(1)}, u32[]{:S(2)}) copy-start(bf16[2048,384]{0,1:T(8,128)(2,1)S(1)} %copy.103) | copy-start | bytes 4718596
  38.8 6.1 %copy-start.2 = (bf16[4,512,6,64]{1,0,3,2:T(4,128)(2,1)}, bf16[4,512,6,64]{1,0,3,2:T(4,128)(2,1)S(1)}, u32[]{:S(2)}) copy-start(bf16[4,512,6,64]{1,0,3,2:T(4,128)(2,1)S(1)} %reshape.128) | copy-start | bytes 4718596
  44.9 4.4 %copy-start.6 = (bf16[2048,128]{1,0:T(8,128)(2,1)S(1)}, bf16[2048,128]{1,0:T(8,128)(2,1)}, u32[]{:S(2)}) copy-start(bf16[2048,128]{1,0:T(8,128)(2,1)} %param.13) | copy-start | bytes 1572868
  49.3 55.1 %copy-start.10 = (f32[6]{0:T(128)S(1)}, f32[6]{0:T(128)}, u32[]{:S(2)}) copy-start(f32[6]{0:T(128)} %copy-done.9) | copy-start | bytes 76
  49.4 55.1 %copy-start.12 = (f32[6]{0:T(128)S(1)}, f32[6]{0:T(128)}, u32[]{:S(2)}) copy-start(f32[6]{0:T(128)} %copy-done.11) | copy-start | bytes 76
  49.4 55.1 %copy-start.13 = (f32[6]{0:T(128)S(1)}, f32[6]{0:T(128)}, u32[]{:S(2)}) copy-start(f32[6]{0:T(128)} %get-tuple-element.158) | copy-start | bytes 76
  49.4 55.1 %copy-start.14 = (f32[6]{0:T(128)S(1)}, f32[6]{0:T(128)}, u32[]{:S(2)}) copy-start(f32[6]{0:T(128)} %get-tuple-element.159) | copy-start | bytes 76
  49.4 55.1 %copy-start.15 = (f32[6]{0:T(128)S(1)}, f32[6]{0:T(128)}, u32[]{:S(2)}) copy-start(f32[6]{0:T(128)} %get-tuple-element.217) | copy-start | bytes 76
  49.4 55.1 %copy-start.16 = (f32[6]{0:T(128)S(1)}, f32[6]{0:T(128)}, u32[]{:S(2)}) copy-start(f32[6]{0:T(128)} %get-tuple-element.218) | copy-start | bytes 76
  104.5 21.0 %copy-start.3 = (bf16[4,512,6,64]{1,0,3,2:T(4,128)(2,1)S(1)}, bf16[4,512,6,64]{1,0,3,2:T(4,128)(2,1)}, u32[]{:S(2)}) copy-start(bf16[4,512,6,64]{1,0,3,2:T(4,128)(2,1)} %copy-done.2) | copy-start | bytes 4718596
  104.5 21.0 %copy-start.7 = (f32[4,512,6,64]{1,3,2,0:T(8,128)S(1)}, f32[4,512,6,64]{1,3,2,0:T(8,128)}, u32[]{:S(2)}) copy-start(f32[4,512,6,64]{1,3,2,0:T(8,128)} %get-tuple-element.70) | copy-start | bytes 9437188
  104.5 21.0 %copy-start.17 = (f32[6]{0:T(128)S(1)}, f32[6]{0:T(128)}, u32[]{:S(2)}) copy-start(f32[6]{0:T(128)} %param.17) | copy-start | bytes 76
  129.7 1.5 copy-start.1
  129.7 2.4 %copy-start.5 = (f32[2048,384]{0,1:T(8,128)S(1)}, f32[2048,384]{0,1:T(8,128)}, u32[]{:S(2)}) copy-start(f32[2048,384]{0,1:T(8,128)} %get-tuple-element.196) | copy-start | bytes 9437188
  148.1 30.7 %collective-permute-start.1 = (f32[3,384]{0,1:T(8,128)}, f32[3,384]{0,1:T(8,128)S(1)}, u32[]{:S(2)}, u32[]{:S(2)}) collective-permute-start(f32[3,384]{0,1:T(8,128)} %slice.143), channel_id=1, source_target_pairs={{4,0},{8,4},{12,8},{5,1},{9,5},{13,9},{6,2},{10,6},{14,10},{7,3},{... | collective-permute-start | bytes 13832 | tf_op jit(solution)/shard_map/ppermute | solution.py:12
  174.6 4.2 %copy-start.4 = (f32[2048,384]{0,1:T(8,128)S(1)}, f32[2048,384]{0,1:T(8,128)}, u32[]{:S(2)}) copy-start(f32[2048,384]{0,1:T(8,128)} %get-tuple-element.186) | copy-start | bytes 9437188
where the time goes:
time: 188 us; the launch traced here: 186 us
  matrix products  60.7 us (32%)
  blocking collectives  56 us (30%)
  local copies, waits for them, and re-layouts  34.3 us (18%)
  other arithmetic  27.2 us (14%)
  starting transfers between devices  6.2 us (3%)
    all_gather x1, blocking collectives, shards(): end_pieces = lax.all_gather(local_end[None], 'seq', axis=0, tiled=True)  18.7 us
    all_gather x1, blocking collectives, shards(): start_pieces = lax.all_gather(running[None], 'seq', axis=0, tiled=True)  17.3 us
    dot_general x4, matrix products, local_block(): jnp.einsum('hst,shp->thp', weights, grad_b, preferred_element_type=jnp.fl...  15.7 us
    dot_general x4, matrix products, local_block(): jnp.einsum('hts,shp->thp', weights, mixed_b, preferred_element_type=jnp.f...  15.7 us
    unnamed x46, local copies, waits for them, and re-layouts  15.7 us
    psum x1, blocking collectives, shards(): lax.psum(local_grad, 'seq') * (row_count * lax.axis_size('seq')) ** (-0.5)  10.1 us
    unnamed x1, blocking collectives  9.92 us
    dot_general x4, matrix products, local_block(): jnp.einsum('thp,tn->hpn', scaled_in, b_block, preferred_element_type=jnp....  7.97 us
  transfers between devices with their start and end apart: 2, of which 0 were waited for; matrix products, arithmetic and copies ran while one was open for 18% of the time, Pallas kernels for 0%

commit v1 on v0

--- a/solution.py
+++ b/solution.py
@@ -4,6 +4,22 @@
 from jax.sharding import PartitionSpec as P
 
 BLOCK = 512
+
+
+def ring_product(x, axis, dim, contribution):
+    size, index, span = (lax.axis_size(axis), lax.axis_index(axis), x.shape[dim])
+    right = [(i, (i + 1) % size) for i in range(size)]
+    left = [(i, (i - 1) % size) for i in range(size)]
+    half = size // 2
+    from_left = from_right = x
+    subtotal = contribution(x, index * span)
+    for hop in range(1, half + 1):
+        from_left = lax.ppermute(from_left, axis, right)
+        if hop < size - half:
+            from_right = lax.ppermute(from_right, axis, left)
+            subtotal = subtotal + contribution(from_right, (index + hop) % size * span)
+        subtotal = subtotal + contribution(from_left, (index - hop) % size * span)
+    return subtotal
 
 
 def shifted(block, axis, distance):
@@ -110,7 +126,6 @@
     prefix = jnp.cumsum(totals_all, axis=0) - totals_all
     own_prefix = lax.dynamic_slice_in_dim(prefix, position, 1, 0)[0]
     end_pieces = lax.all_gather(local_end[None], "seq", axis=0, tiled=True)
-    start_pieces = lax.all_gather(running[None], "seq", axis=0, tiled=True)
     piece_count = end_pieces.shape[0]
     sources = jnp.arange(piece_count, dtype=jnp.int32)
     from_below = (sources < position)[:, None]
@@ -122,7 +137,17 @@
         jnp.where(from_above, prefix - own_prefix[None] - device_total[None], -jnp.inf)
     )
     forward_sum = jnp.einsum("jh,jhpn->hpn", forward_weight, end_pieces, precision=highest)
-    backward_sum = jnp.einsum("jh,jhpn->hpn", backward_weight, start_pieces, precision=highest)
+    backward_sum = ring_product(
+        running[None],
+        "seq",
+        0,
+        lambda part, start: jnp.einsum(
+            "jh,jhpn->hpn",
+            lax.dynamic_slice_in_dim(backward_weight, start, part.shape[0], axis=0),
+            part,
+            precision=highest,
+        ),
+    )
     before_blocks = jnp.cumsum(block_totals, axis=0) - block_totals
     after_blocks = device_total[None] - jnp.cumsum(block_totals, axis=0)
     start_states = jnp.exp(before_blocks)[:, :, None, None] * forward_sum[None] + jnp.stack(

time: 188 us -> 185 us (0.984)
  blocking collectives: 56 us -> 43.1 us
  other arithmetic: 27.2 us -> 33.2 us
  starting transfers between devices: 6.2 us -> 10.3 us
  matrix products: 60.7 us -> 58.7 us
    all_gather x1 -> x0, blocking collectives: 17.3 us -> none  [shards(): start_pieces = lax.all_gather(running[None], 'seq', axis=0, tiled=True)]
    convert_element_type x1, other arithmetic: 5.04 us -> 9.42 us  [shards(): return (layer_out, input_grad.astype(jnp.bfloat16), conv_grad)]
    ppermute x0 -> x3, starting transfers between devices: none -> 4.06 us  [the longest x1 3.21 us: ring_product(): from_right = lax.ppermute(from_right, axis, left)]
    all_gather x1, blocking collectives: 18.7 us -> 21.1 us  [shards(): end_pieces = lax.all_gather(local_end[None], 'seq', axis=0, tiled=True)]
    psum x1, blocking collectives: 10.1 us -> 12 us  [shards(): lax.psum(local_grad, 'seq') * (row_count * lax.axis_size('seq')) ** (-0.5)]
    unnamed x46 -> x56, local copies, waits for them, and re-layouts: 15.7 us -> 15.8 us
  transfers between devices with their start and end apart: 2 -> 5, of which waited for: 0 -> 1; matrix products, arithmetic and copies ran while one was open for 18% -> 19% of each run, Pallas kernels for 0% -> 0%
where the time goes in v1:
time: 185 us; the launch traced here: 184 us
  matrix products  58.7 us (32%)
  blocking collectives  43.1 us (23%)
  local copies, waits for them, and re-layouts  35.3 us (19%)
  other arithmetic  33.2 us (18%)
  starting transfers between devices  10.3 us (6%)
    all_gather x1, blocking collectives, shards(): end_pieces = lax.all_gather(local_end[None], 'seq', axis=0, tiled=True)  21.1 us
    unnamed x56, local copies, waits for them, and re-layouts  15.8 us
    dot_general x4, matrix products, local_block(): jnp.einsum('hts,shp->thp', weights, mixed_b, preferred_element_type=jnp.f...  15.7 us
    dot_general x4, matrix products, local_block(): jnp.einsum('hst,shp->thp', weights, grad_b, preferred_element_type=jnp.fl...  15.7 us
    psum x1, blocking collectives, shards(): lax.psum(local_grad, 'seq') * (row_count * lax.axis_size('seq')) ** (-0.5)  12 us
    unnamed x1, blocking collectives  9.92 us
    convert_element_type x1, other arithmetic, shards(): return (layer_out, input_grad.astype(jnp.bfloat16), conv_grad)  9.42 us
    dot_general x4, matrix products, local_block(): jnp.einsum('thp,tn->hpn', scaled_in, b_block, preferred_element_type=jnp....  7.96 us
  transfers between devices with their start and end apart: 5, of which 1 were waited for; matrix products, arithmetic and copies ran while one was open for 19% of the time, Pallas kernels for 0%

profile of v1, /device:TPU:0, one launch (start us, length us, event | category | flops | bytes accessed | tf_op | source)
XLA Modules:
  0.0 183.8 jit_solution(16388418348041469794)
XLA Ops:
  0.6 0.8 slice.104
  1.5 0.8 copy.102
  2.2 4.9 %collective-permute-start = (bf16[3,384]{0,1:T(8,128)(2,1)}, bf16[3,384]{0,1:T(8,128)(2,1)S(1)}, u32[]{:S(2)}, u32[]{:S(2)}) collective-permute-start(bf16[3,384]{0,1:T(8,128)(2,1)} %copy.102), channel_id=1, source_target_pairs={{0,4},{4,8},{8,12},{1,5},{5,9},{9,13},{2,6},{6,10},{10,14},{3,7},{... | collective-permute-start | bytes 6920 | tf_op jit(solution)/shard_map/ppermute | solution.py:28
  7.2 0.7 subtract_log_fusion
  7.9 0.7 neg.13
  8.5 0.9 multiply_exponential_fusion
  9.5 7.2 %reduce-window.6 = f32[6,4,4,128]{3,2,1,0:T(4,128)S(1)} reduce-window(f32[6,4,4,128]{3,2,1,0:T(4,128)S(1)} %reshape.149, f32[]{:T(128)} %constant.72.clone.1), window={size=1x1x1x128 pad=0_0x0_0x0_0x127_0}, to_apply=%region_0.1 | reduce-window | flops 1560576 | bytes 98308 | tf_op jit(solution)/shard_map/reduce-window
  17.5 0.8 fusion.74
  18.6 0.9 slice_reduce_fusion.3
  19.5 1.2 dynamic-slice
  21.7 9.9 %all-reduce = f32[24]{0:T(128)S(1)} all-reduce(f32[24]{0:T(128)S(1)} %dynamic-update-slice), channel_id=2, replica_groups=mesh['groups'=2,'seq'=4,'head'=2,'sub'=2] {'seq'}, use_global_device_ids=true, to_apply=%add | all-reduce | flops 24 | bytes 192
  32.4 0.6 subtract_exponential_fusion
  33.0 0.6 fusion.79
  33.6 1.7 copy.103
  35.4 1.6 copy.108
  37.0 2.9 %reshape.152 = bf16[4,512,6,64]{1,0,3,2:T(4,128)(2,1)S(1)} reshape(bf16[2048,384]{0,1:T(8,128)(2,1)} %copy.108) | data formatting | bytes 3145728 | tf_op jit(solution)/shard_map/reshape | solution.py:67
  39.9 1.7 copy.112
  41.5 0.6 copy.114
  42.2 0.7 copy.122
  42.8 0.6 copy.118
  43.5 4.2 %multiply_convert_fusion.13 = (bf16[2048,384]{0,1:T(8,128)(2,1)}, f32[2048,384]{0,1:T(8,128)}) fusion(bf16[2048,384]{0,1:T(8,128)(2,1)S(1)} %copy.103, f32[384]{0:T(512)S(1)} %get-tuple-element.162, bf16[3,384]{0,1:T(8,128)(2,1)S(1)} %collective-permute-done, f32[384]{0:T(512)S(1)} %get-tuple-element.163, f32[384]{0:T(512)S(1)} %get-tuple-element.161, ...), kind=kLoop, calls=%fused_computation.84 | loop fusion | flops 19660800 | bytes 6299904 | tf_op jit(solution)/shard_map/convert_element_type | solution.py:56
  47.7 2.9 %reshape.146 = bf16[4,512,6,64]{1,0,3,2:T(4,128)(2,1)S(1)} reshape(bf16[2048,384]{0,1:T(8,128)(2,1)} %get-tuple-element.195) | data formatting | bytes 3145728 | tf_op jit(solution)/shard_map/reshape | solution.py:66
  50.6 1.7 copy.105
  52.3 55.5 %while.17 = (s32[]{:T(128)}, f32[4,512,6,64]{1,3,2,0:T(8,128)}, f32[4,512,6,64]{1,3,2,0:T(8,128)}, f32[4,6,64,128]{3,2,1,0:T(8,128)}, f32[4,6,64,128]{3,2,1,0:T(...) while((s32[]{:T(128)}, f32[4,512,6,64]{1,3,2,0:T(8,128)}, ...), condition=%wide.region_3.4_spmd.clone, body=%wide.region_2.3_spmd.clone.sunk | while | flops 587601920 | bytes 8370377 | solution.py:98
  52.4 1.3 fusion.111
  53.7 3.9 %fusion.112 = f32[4,512,6,64]{1,3,2,0:T(8,128)} fusion(f32[4,512,6,64]{1,3,2,0:T(8,128)} %get-tuple-element.313, s32[]{:T(128)S(6)} %copy.162, f32[6,512]{1,0:T(8,128)S(1)} %bitcast.199, f32[6,512]{1,0:T(8,128)S(1)} %bitcast.201, f32[512,512]{1,0:T(8,128)S(1)} %fusion.111, pred[512,512]{1,0:T(8,128)(4,1)S(1)} %iota_compare_fusion.4, ...), kind=kOutput, calls=%fused_computation.5.clone.1 | convolution fusion | flops 209190912 | bytes 2540544 | tf_op jit(solution)/shard_map/while/body/eval_jaxpr/hts,shp->thp/dot_general | solution.py:78
  57.6 3.9 %fusion.113 = f32[4,512,6,64]{1,3,2,0:T(8,128)} fusion(f32[4,512,6,64]{1,3,2,0:T(8,128)} %get-tuple-element.314, s32[]{:T(128)S(6)} %copy.162, f32[6,512]{1,0:T(8,128)S(1)} %bitcast.200, f32[6,512]{1,0:T(8,128)S(1)} %bitcast.202, f32[512,512]{1,0:T(8,128)S(1)} %fusion.111, pred[512,512]{1,0:T(8,128)(4,1)S(1)} %iota_compare_fusion.4, ...), kind=kOutput, calls=%fused_computation.7.clone.1 | convolution fusion | flops 209190912 | bytes 2540544 | tf_op jit(solution)/shard_map/while/body/eval_jaxpr/hst,shp->thp/dot_general | solution.py:81
  62.1 2.0 %fusion.114 = f32[4,6,64,128]{3,2,1,0:T(8,128)} fusion(f32[4,6,64,128]{3,2,1,0:T(8,128)} %get-tuple-element.315, s32[]{:T(128)S(6)} %copy.162, f32[512,6]{0,1:T(8,128)S(1)} %copy.151, bf16[4,512,6,64]{1,3,2,0:T(8,128)(2,1)} %get-tuple-element.329, bf16[4,512,128]{2,1,0:T(8,128)(2,1)} %get-tuple-element.331), kind=kOutput, calls=%fused_computation.11.clone.1 | convolution fusion | flops 50921472 | bytes 734720 | tf_op jit(solution)/shard_map/while/body/eval_jaxpr/thp,tn->hpn/dot_general | solution.py:87
  64.2 2.0 %fusion.115 = f32[4,6,64,128]{3,2,1,0:T(8,128)} fusion(f32[4,6,64,128]{3,2,1,0:T(8,128)} %get-tuple-element.316, s32[]{:T(128)S(6)} %copy.162, f32[512,6]{0,1:T(8,128)S(1)} %copy.152, bf16[4,512,6,64]{1,3,2,0:T(8,128)(2,1)} %get-tuple-element.334, bf16[4,512,128]{2,1,0:T(8,128)(2,1)} %get-tuple-element.330), kind=kOutput, calls=%fused_computation.9.clone.1 | convolution fusion | flops 50921472 | bytes 734720 | tf_op jit(solution)/shard_map/while/body/eval_jaxpr/thp,tn->hpn/dot_general | solution.py:93
  66.2 1.3 fusion.111
  67.6 3.9 %fusion.112 = f32[4,512,6,64]{1,3,2,0:T(8,128)} fusion(f32[4,512,6,64]{1,3,2,0:T(8,128)} %get-tuple-element.313, s32[]{:T(128)S(6)} %copy.162, f32[6,512]{1,0:T(8,128)S(1)} %bitcast.199, f32[6,512]{1,0:T(8,128)S(1)} %bitcast.201, f32[512,512]{1,0:T(8,128)S(1)} %fusion.111, pred[512,512]{1,0:T(8,128)(4,1)S(1)} %iota_compare_fusion.4, ...), kind=kOutput, calls=%fused_computation.5.clone.1 | convolution fusion | flops 209190912 | bytes 2540544 | tf_op jit(solution)/shard_map/while/body/eval_jaxpr/hts,shp->thp/dot_general | solution.py:78
  71.5 3.9 %fusion.113 = f32[4,512,6,64]{1,3,2,0:T(8,128)} fusion(f32[4,512,6,64]{1,3,2,0:T(8,128)} %get-tuple-element.314, s32[]{:T(128)S(6)} %copy.162, f32[6,512]{1,0:T(8,128)S(1)} %bitcast.200, f32[6,512]{1,0:T(8,128)S(1)} %bitcast.202, f32[512,512]{1,0:T(8,128)S(1)} %fusion.111, pred[512,512]{1,0:T(8,128)(4,1)S(1)} %iota_compare_fusion.4, ...), kind=kOutput, calls=%fused_computation.7.clone.1 | convolution fusion | flops 209190912 | bytes 2540544 | tf_op jit(solution)/shard_map/while/body/eval_jaxpr/hst,shp->thp/dot_general | solution.py:81
  75.9 2.0 %fusion.114 = f32[4,6,64,128]{3,2,1,0:T(8,128)} fusion(f32[4,6,64,128]{3,2,1,0:T(8,128)} %get-tuple-element.315, s32[]{:T(128)S(6)} %copy.162, f32[512,6]{0,1:T(8,128)S(1)} %copy.151, bf16[4,512,6,64]{1,3,2,0:T(8,128)(2,1)} %get-tuple-element.329, bf16[4,512,128]{2,1,0:T(8,128)(2,1)} %get-tuple-element.331), kind=kOutput, calls=%fused_computation.11.clone.1 | convolution fusion | flops 50921472 | bytes 734720 | tf_op jit(solution)/shard_map/while/body/eval_jaxpr/thp,tn->hpn/dot_general | solution.py:87
  78.0 2.0 %fusion.115 = f32[4,6,64,128]{3,2,1,0:T(8,128)} fusion(f32[4,6,64,128]{3,2,1,0:T(8,128)} %get-tuple-element.316, s32[]{:T(128)S(6)} %copy.162, f32[512,6]{0,1:T(8,128)S(1)} %copy.152, bf16[4,512,6,64]{1,3,2,0:T(8,128)(2,1)} %get-tuple-element.334, bf16[4,512,128]{2,1,0:T(8,128)(2,1)} %get-tuple-element.330), kind=kOutput, calls=%fused_computation.9.clone.1 | convolution fusion | flops 50921472 | bytes 734720 | tf_op jit(solution)/shard_map/while/body/eval_jaxpr/thp,tn->hpn/dot_general | solution.py:93
  80.0 1.3 fusion.111
  81.4 4.0 %fusion.112 = f32[4,512,6,64]{1,3,2,0:T(8,128)} fusion(f32[4,512,6,64]{1,3,2,0:T(8,128)} %get-tuple-element.313, s32[]{:T(128)S(6)} %copy.162, f32[6,512]{1,0:T(8,128)S(1)} %bitcast.199, f32[6,512]{1,0:T(8,128)S(1)} %bitcast.201, f32[512,512]{1,0:T(8,128)S(1)} %fusion.111, pred[512,512]{1,0:T(8,128)(4,1)S(1)} %iota_compare_fusion.4, ...), kind=kOutput, calls=%fused_computation.5.clone.1 | convolution fusion | flops 209190912 | bytes 2540544 | tf_op jit(solution)/shard_map/while/body/eval_jaxpr/hts,shp->thp/dot_general | solution.py:78
  85.3 3.9 %fusion.113 = f32[4,512,6,64]{1,3,2,0:T(8,128)} fusion(f32[4,512,6,64]{1,3,2,0:T(8,128)} %get-tuple-element.314, s32[]{:T(128)S(6)} %copy.162, f32[6,512]{1,0:T(8,128)S(1)} %bitcast.200, f32[6,512]{1,0:T(8,128)S(1)} %bitcast.202, f32[512,512]{1,0:T(8,128)S(1)} %fusion.111, pred[512,512]{1,0:T(8,128)(4,1)S(1)} %iota_compare_fusion.4, ...), kind=kOutput, calls=%fused_computation.7.clone.1 | convolution fusion | flops 209190912 | bytes 2540544 | tf_op jit(solution)/shard_map/while/body/eval_jaxpr/hst,shp->thp/dot_general | solution.py:81
  89.8 2.0 %fusion.114 = f32[4,6,64,128]{3,2,1,0:T(8,128)} fusion(f32[4,6,64,128]{3,2,1,0:T(8,128)} %get-tuple-element.315, s32[]{:T(128)S(6)} %copy.162, f32[512,6]{0,1:T(8,128)S(1)} %copy.151, bf16[4,512,6,64]{1,3,2,0:T(8,128)(2,1)} %get-tuple-element.329, bf16[4,512,128]{2,1,0:T(8,128)(2,1)} %get-tuple-element.331), kind=kOutput, calls=%fused_computation.11.clone.1 | convolution fusion | flops 50921472 | bytes 734720 | tf_op jit(solution)/shard_map/while/body/eval_jaxpr/thp,tn->hpn/dot_general | solution.py:87
  91.9 2.0 %fusion.115 = f32[4,6,64,128]{3,2,1,0:T(8,128)} fusion(f32[4,6,64,128]{3,2,1,0:T(8,128)} %get-tuple-element.316, s32[]{:T(128)S(6)} %copy.162, f32[512,6]{0,1:T(8,128)S(1)} %copy.152, bf16[4,512,6,64]{1,3,2,0:T(8,128)(2,1)} %get-tuple-element.334, bf16[4,512,128]{2,1,0:T(8,128)(2,1)} %get-tuple-element.330), kind=kOutput, calls=%fused_computation.9.clone.1 | convolution fusion | flops 50921472 | bytes 734720 | tf_op jit(solution)/shard_map/while/body/eval_jaxpr/thp,tn->hpn/dot_general | solution.py:93
  93.9 1.3 fusion.111
  95.3 3.9 %fusion.112 = f32[4,512,6,64]{1,3,2,0:T(8,128)} fusion(f32[4,512,6,64]{1,3,2,0:T(8,128)} %get-tuple-element.313, s32[]{:T(128)S(6)} %copy.162, f32[6,512]{1,0:T(8,128)S(1)} %bitcast.199, f32[6,512]{1,0:T(8,128)S(1)} %bitcast.201, f32[512,512]{1,0:T(8,128)S(1)} %fusion.111, pred[512,512]{1,0:T(8,128)(4,1)S(1)} %iota_compare_fusion.4, ...), kind=kOutput, calls=%fused_computation.5.clone.1 | convolution fusion | flops 209190912 | bytes 2540544 | tf_op jit(solution)/shard_map/while/body/eval_jaxpr/hts,shp->thp/dot_general | solution.py:78
  99.2 4.0 %fusion.113 = f32[4,512,6,64]{1,3,2,0:T(8,128)} fusion(f32[4,512,6,64]{1,3,2,0:T(8,128)} %get-tuple-element.314, s32[]{:T(128)S(6)} %copy.162, f32[6,512]{1,0:T(8,128)S(1)} %bitcast.200, f32[6,512]{1,0:T(8,128)S(1)} %bitcast.202, f32[512,512]{1,0:T(8,128)S(1)} %fusion.111, pred[512,512]{1,0:T(8,128)(4,1)S(1)} %iota_compare_fusion.4, ...), kind=kOutput, calls=%fused_computation.7.clone.1 | convolution fusion | flops 209190912 | bytes 2540544 | tf_op jit(solution)/shard_map/while/body/eval_jaxpr/hst,shp->thp/dot_general | solution.py:81
  103.7 2.0 %fusion.114 = f32[4,6,64,128]{3,2,1,0:T(8,128)} fusion(f32[4,6,64,128]{3,2,1,0:T(8,128)} %get-tuple-element.315, s32[]{:T(128)S(6)} %copy.162, f32[512,6]{0,1:T(8,128)S(1)} %copy.151, bf16[4,512,6,64]{1,3,2,0:T(8,128)(2,1)} %get-tuple-element.329, bf16[4,512,128]{2,1,0:T(8,128)(2,1)} %get-tuple-element.331), kind=kOutput, calls=%fused_computation.11.clone.1 | convolution fusion | flops 50921472 | bytes 734720 | tf_op jit(solution)/shard_map/while/body/eval_jaxpr/thp,tn->hpn/dot_general | solution.py:87
  105.8 2.0 %fusion.115 = f32[4,6,64,128]{3,2,1,0:T(8,128)} fusion(f32[4,6,64,128]{3,2,1,0:T(8,128)} %get-tuple-element.316, s32[]{:T(128)S(6)} %copy.162, f32[512,6]{0,1:T(8,128)S(1)} %copy.152, bf16[4,512,6,64]{1,3,2,0:T(8,128)(2,1)} %get-tuple-element.334, bf16[4,512,128]{2,1,0:T(8,128)(2,1)} %get-tuple-element.330), kind=kOutput, calls=%fused_computation.9.clone.1 | convolution fusion | flops 50921472 | bytes 734720 | tf_op jit(solution)/shard_map/while/body/eval_jaxpr/thp,tn->hpn/dot_general | solution.py:93
  107.9 2.6 %slice_add_fusion = (f32[1,6,64,128]{3,2,1,0:T(8,128)S(1)}, f32[1,6,64,128]{3,2,1,0:T(8,128)}, f32[1,6,64,128]{3,2,1,0:T(8,128)}, f32[1,6,64,128]{3,2,1,0:T(8,12...) fusion(f32[4,6,64,128]{3,2,1,0:T(8,128)} %get-tuple-element.71,, ...), kind=kLoop, calls=%fused_computation.108 | loop fusion | flops 688128 | bytes 3145872 | tf_op jit(solution)/shard_map/add | solution.py:119
  110.4 0.6 collective-permute-start.2
  111.0 3.2 %collective-permute-start.1 = (f32[1,6,64,128]{3,2,1,0:T(8,128)S(1)}, f32[1,6,64,128]{3,2,1,0:T(8,128)}, u32[]{:S(2)}, u32[]{:S(2)}) collective-permute-start(f32[1,6,64,128]{3,2,1,0:T(8,128)S(1)} %get-tuple-element.187), channel_id=1, source_target_pairs={{0,12},{4,0},{8,4},{12,8},{1,13},{5,1},{9,5},{13,9},{2,14},{6,2},{... | collective-permute-start | bytes 589832 | tf_op jit(solution)/shard_map/ppermute | solution.py:19
  114.2 21.1 %all_gather.7 = f32[4,6,64,128]{3,2,1,0:T(8,128)S(1)} all-gather(f32[1,6,64,128]{3,2,1,0:T(8,128)S(1)} %get-tuple-element.215), channel_id=1, replica_groups=mesh['groups'=2,'seq'=4,'head'=2,'sub'=2] {'seq'}, dimensions={0}, use_global_device_ids=true | all-gather | bytes 983040 | tf_op jit(solution)/shard_map/all_gather | solution.py:128
  135.4 1.8 fusion.62
  137.6 1.2 fusion.57
  138.7 1.2 copy.115
  140.0 1.6 copy.131
  141.5 2.6 %copy.120 = bf16[2048,384]{1,0:T(8,128)(2,1)} copy(bf16[2048,384]{0,1:T(8,128)(2,1)} %bitcast.193) | data formatting | bytes 3145728
  144.1 1.1 collective-permute-done.3
  145.2 1.2 fusion.70
  146.5 3.3 %fusion.55 = f32[4,512,6,64]{1,3,2,0:T(8,128)S(1)} fusion(f32[4,512,6,64]{1,3,2,0:T(8,128)} %get-tuple-element.70, bf16[4,512,128,1]{2,1,3,0:T(8,128)(2,1)} %bitcast.191, f32[4,512,6]{1,2,0:T(8,128)} %copy.118, f32[6]{0:T(128)} %param.17, f32[1,6,64,128]{3,2,1,0:T(8,128)S(1)} %broadcast.80, f32[1,6,64,128]{3,2,1,0:T(8,128)} %get-tuple-element.190, ...), kind=kOutput, calls=%fused_computation.79 | convolution fusion | flops 206438400 | bytes 9420920 | tf_op jit(solution)/shard_map/btn,bhpn->bthp/dot_general | solution.py:172
  149.8 2.0 %copy.119 = f32[4,512,6,64]{1,0,3,2:T(4,128)S(1)} copy(f32[4,512,6,64]{1,3,2,0:T(8,128)S(1)} %fusion.55) | data formatting | bytes 6291456 | tf_op jit(solution)/shard_map/add | solution.py:179
  151.9 1.5 copy.132
  153.8 3.3 %fusion.50 = (f32[384]{0:T(512)S(1)}, f32[384]{0:T(512)S(1)}, f32[384]{0:T(512)S(1)}, f32[384]{0:T(512)S(1)}, f32[2048,384]{0,1:T(8,128)S(1)}) fusion(bf16[2048,384]{0,1:T(8,128)(2,1)S(1)} %copy.103, bf16[3,384]{0,1:T(8,128)(2,1)S(1)} %copy-done.10, f32[2048,384]{0,1:T(8,128)S(1)} %copy-done.5, f32[2048,384]{0,1:T(8,128)S(1)} %bitcast.187), kind=kLoop, calls=%fused_computation.72 | loop fusion | flops 22804992 | bytes 11018496 | tf_op jit(solution)/shard_map/reduce_sum | solution.py:193
  157.1 1.7 copy-done.4
  158.8 1.3 collective-permute-start.4
  160.1 12.0 %psum.7 = f32[4,384]{1,0:T(4,128)S(1)} all-reduce(f32[4,384]{1,0:T(4,128)S(1)} %pad_maximum_fusion.2), channel_id=1, replica_groups=mesh['groups'=2,'seq'=4,'head'=2,'sub'=2] {'seq'}, use_global_device_ids=true, to_apply=%region_11.12 | all-reduce | flops 1536 | bytes 12288 | tf_op jit(solution)/shard_map/psum | solution.py:197
  172.8 9.4 %fusion.44 = bf16[2048,384]{0,1:T(8,128)(2,1)S(1)} fusion(f32[2048,384]{0,1:T(8,128)} %copy-done.4, f32[3,384]{0,1:T(8,128)S(1)} %collective-permute-done.4, f32[384]{0:T(512)S(1)} %get-tuple-element.162, f32[384]{0:T(512)S(1)} %get-tuple-element.163, f32[384]{0:T(512)S(1)} %get-tuple-element.161, f32[384]{0:T(512)S(1)} %get-tuple-element.160), kind=kLoop, calls=%fused_computation.66 | loop fusion | flops 8650752 | bytes 4729344 | tf_op jit(solution)/shard_map/convert_element_type | solution.py:198
  182.2 1.6 copy.121
  (124 shorter events, 6.4 us)
Async XLA Ops:
  0.6 34.7 %copy-start.8 = (bf16[2048,384]{1,0:T(8,128)(2,1)S(1)}, bf16[2048,384]{1,0:T(8,128)(2,1)}, u32[]{:S(2)}) copy-start(bf16[2048,384]{1,0:T(8,128)(2,1)} %param.19) | copy-start | bytes 4718596
  2.2 41.2 %collective-permute-start = (bf16[3,384]{0,1:T(8,128)(2,1)}, bf16[3,384]{0,1:T(8,128)(2,1)S(1)}, u32[]{:S(2)}, u32[]{:S(2)}) collective-permute-start(bf16[3,384]{0,1:T(8,128)(2,1)} %copy.102), channel_id=1, source_target_pairs={{0,4},{4,8},{8,12},{1,5},{5,9},{9,13},{2,6},{6,10},{10,14},{3,7},{... | collective-permute-start | bytes 6920 | tf_op jit(solution)/shard_map/ppermute | solution.py:28
  18.3 15.3 %copy-start.14 = (f32[6]{0:T(128)}, f32[6]{0:T(128)S(1)}, u32[]{:S(2)}) copy-start(f32[6]{0:T(128)S(1)} %get-tuple-element.156) | copy-start | bytes 76
  18.3 15.3 %copy-start.16 = (f32[6]{0:T(128)}, f32[6]{0:T(128)S(1)}, u32[]{:S(2)}) copy-start(f32[6]{0:T(128)S(1)} %get-tuple-element.157) | copy-start | bytes 76
  39.9 7.8 %copy-start.2 = (bf16[4,512,6,64]{1,0,3,2:T(4,128)(2,1)}, bf16[4,512,6,64]{1,0,3,2:T(4,128)(2,1)S(1)}, u32[]{:S(2)}) copy-start(bf16[4,512,6,64]{1,0,3,2:T(4,128)(2,1)S(1)} %reshape.152) | copy-start | bytes 4718596
  43.5 4.2 %copy-start.9 = (bf16[3,384]{0,1:T(8,128)(2,1)}, bf16[3,384]{0,1:T(8,128)(2,1)S(1)}, u32[]{:S(2)}) copy-start(bf16[3,384]{0,1:T(8,128)(2,1)S(1)} %collective-permute-done) | copy-start | bytes 6916
  50.6 1.7 copy-start
  52.2 55.6 %copy-start.15 = (f32[6]{0:T(128)S(1)}, f32[6]{0:T(128)}, u32[]{:S(2)}) copy-start(f32[6]{0:T(128)} %copy-done.14) | copy-start | bytes 76
  52.2 55.6 %copy-start.17 = (f32[6]{0:T(128)S(1)}, f32[6]{0:T(128)}, u32[]{:S(2)}) copy-start(f32[6]{0:T(128)} %copy-done.16) | copy-start | bytes 76
  52.2 55.6 %copy-start.18 = (f32[6]{0:T(128)S(1)}, f32[6]{0:T(128)}, u32[]{:S(2)}) copy-start(f32[6]{0:T(128)} %get-tuple-element.158) | copy-start | bytes 76
  52.2 55.6 %copy-start.19 = (f32[6]{0:T(128)S(1)}, f32[6]{0:T(128)}, u32[]{:S(2)}) copy-start(f32[6]{0:T(128)} %get-tuple-element.159) | copy-start | bytes 76
  52.2 55.6 %copy-start.20 = (f32[6]{0:T(128)S(1)}, f32[6]{0:T(128)}, u32[]{:S(2)}) copy-start(f32[6]{0:T(128)} %get-tuple-element.221) | copy-start | bytes 76
  52.3 55.6 %copy-start.21 = (f32[6]{0:T(128)S(1)}, f32[6]{0:T(128)}, u32[]{:S(2)}) copy-start(f32[6]{0:T(128)} %get-tuple-element.222) | copy-start | bytes 76
  52.3 83.1 %copy-start.12 = (f32[4,6,1,1]{0,2,3,1:T(1,128)S(1)}, f32[4,6,1,1]{0,2,3,1:T(1,128)}, u32[]{:S(2)}) copy-start(f32[4,6,1,1]{0,2,3,1:T(1,128)} %copy.122) | copy-start | bytes 292
  107.8 29.7 %copy-start.1 = (bf16[4,512,6,64]{1,0,3,2:T(4,128)(2,1)S(1)}, bf16[4,512,6,64]{1,0,3,2:T(4,128)(2,1)}, u32[]{:S(2)}) copy-start(bf16[4,512,6,64]{1,0,3,2:T(4,128)(2,1)} %copy-done) | copy-start | bytes 4718596
  107.8 29.7 %copy-start.6 = (bf16[4,512,128]{2,1,0:T(8,128)(2,1)S(1)}, bf16[4,512,128]{2,1,0:T(8,128)(2,1)}, u32[]{:S(2)}) copy-start(bf16[4,512,128]{2,1,0:T(8,128)(2,1)} %get-tuple-element.336) | copy-start | bytes 1572868
  107.8 29.7 %copy-start.7 = (f32[4,512,6,64]{1,3,2,0:T(8,128)S(1)}, f32[4,512,6,64]{1,3,2,0:T(8,128)}, u32[]{:S(2)}) copy-start(f32[4,512,6,64]{1,3,2,0:T(8,128)} %get-tuple-element.68) | copy-start | bytes 9437188
  107.8 29.7 %copy-start.11 = (f32[4,512,6]{1,2,0:T(8,128)S(1)}, f32[4,512,6]{1,2,0:T(8,128)}, u32[]{:S(2)}) copy-start(f32[4,512,6]{1,2,0:T(8,128)} %copy.114) | copy-start | bytes 147460
  107.8 29.7 %copy-start.13 = (f32[4,6]{1,0:T(4,128)S(1)}, f32[4,6]{1,0:T(4,128)}, u32[]{:S(2)}) copy-start(f32[4,6]{1,0:T(4,128)} %get-tuple-element.210) | copy-start | bytes 292
  107.8 29.7 %copy-start.22 = (f32[6]{0:T(128)S(1)}, f32[6]{0:T(128)}, u32[]{:S(2)}) copy-start(f32[6]{0:T(128)} %param.17) | copy-start | bytes 76
  110.4 26.8 %collective-permute-start.2 = (f32[1,6,64,128]{3,2,1,0:T(8,128)S(1)}, f32[1,6,64,128]{3,2,1,0:T(8,128)}, u32[]{:S(2)}, u32[]{:S(2)}) collective-permute-start(f32[1,6,64,128]{3,2,1,0:T(8,128)S(1)} %get-tuple-element.187), channel_id=1, source_target_pairs={{0,4},{4,8},{8,12},{12,0},{1,5},{5,9},{9,13},{13,1},{2,6},{6,10},{... | collective-permute-start | bytes 589832 | tf_op jit(solution)/shard_map/ppermute | solution.py:17
  111.0 33.1 %collective-permute-start.1 = (f32[1,6,64,128]{3,2,1,0:T(8,128)S(1)}, f32[1,6,64,128]{3,2,1,0:T(8,128)}, u32[]{:S(2)}, u32[]{:S(2)}) collective-permute-start(f32[1,6,64,128]{3,2,1,0:T(8,128)S(1)} %get-tuple-element.187), channel_id=1, source_target_pairs={{0,12},{4,0},{8,4},{12,8},{1,13},{5,1},{9,5},{13,9},{2,14},{6,2},{... | collective-permute-start | bytes 589832 | tf_op jit(solution)/shard_map/ppermute | solution.py:19
  137.2 8.0 %collective-permute-start.3 = (f32[1,6,64,128]{3,2,1,0:T(8,128)}, f32[1,6,64,128]{3,2,1,0:T(8,128)}, u32[]{:S(2)}, u32[]{:S(2)}) collective-permute-start(f32[1,6,64,128]{3,2,1,0:T(8,128)} %collective-permute-done.2), channel_id=1, source_target_pairs={{0,4},{4,8},{8,12},{12,0},{1,5},{5,9},{9,13},{13,1},{2,6},{6,10},{... | collective-permute-start | bytes 589832 | tf_op jit(solution)/shard_map/ppermute | solution.py:17
  139.9 6.6 %copy-start.3 = (bf16[4,512,6,64]{1,0,3,2:T(4,128)(2,1)S(1)}, bf16[4,512,6,64]{1,0,3,2:T(4,128)(2,1)}, u32[]{:S(2)}) copy-start(bf16[4,512,6,64]{1,0,3,2:T(4,128)(2,1)} %copy-done.2) | copy-start | bytes 4718596
  151.9 1.9 %copy-start.5 = (f32[2048,384]{0,1:T(8,128)S(1)}, f32[2048,384]{0,1:T(8,128)}, u32[]{:S(2)}) copy-start(f32[2048,384]{0,1:T(8,128)} %get-tuple-element.196) | copy-start | bytes 9437188
  151.9 1.9 %copy-start.10 = (bf16[3,384]{0,1:T(8,128)(2,1)S(1)}, bf16[3,384]{0,1:T(8,128)(2,1)}, u32[]{:S(2)}) copy-start(bf16[3,384]{0,1:T(8,128)(2,1)} %copy-done.9) | copy-start | bytes 6916
  157.1 1.7 copy-start.4
  158.8 14.0 %collective-permute-start.4 = (f32[3,384]{0,1:T(8,128)S(1)}, f32[3,384]{0,1:T(8,128)S(1)}, u32[]{:S(2)}, u32[]{:S(2)}) collective-permute-start(f32[3,384]{0,1:T(8,128)S(1)} %slice.143), channel_id=1, source_target_pairs={{4,0},{8,4},{12,8},{5,1},{9,5},{13,9},{6,2},{10,6},{14,10},{7,3},{... | collective-permute-start | bytes 13832 | tf_op jit(solution)/shard_map/ppermute | solution.py:28
